TPU v7x, 32 devices: a whole 2x2x4 slice. The times are simulated.
32 devices in a mesh: row: 4 (over y, core), col: 8 (over z, x).
Axes of the slice: x: 2, y: 2, z: 4, core: 2. Of those that a mesh axis runs over, the one named last changes fastest.
Arguments:
- front: float32 [12288, 12288], P('row', 'col'), may hold values from -6 to 6
- delayed: float32 [64, 12288], P('col', 'row'), may hold values from -6 to 6
- dest: int32 [64], P('col'), may hold values from 0 to 1023, as said below
- pivots: int32 [1024], replicated, may hold values from 0 to 12287, as said below
- pair_flags: int32 [1024], replicated, may hold values from 0 to 1, as said below
- linv: float32 [4, 256, 256], replicated, as said below
- dinv_diag: float32 [1024], replicated, may hold values from -0.1 to 0.1
- dinv_off: float32 [1024], replicated, may hold values from -0.08 to 0.08
Outputs:
- trailing: float32 [12288, 12288], P('row', 'col')
- factor: float32 [12288, 1024], P('row')
Inputs may be any that keep to these rules, and one draw needn't show every extreme that they name: Distinct front columns; slots p * 256 to (p + 1) * 256 - 1 are panel p's pivots. Each block of 1536 columns held by one index of col contains exactly 128 of them. `pair_flags`: A 1 at slot s joins slots s and s + 1 into one 2x2 block; no two 1s are adjacent and the last slot of a panel holds 0. `dest`: several delayed columns may share a slot. Of the 8 delayed columns held by one index of col, at most 2 go to pivot columns held by the same index of col. `linv`: each panel's matrix is unit lower triangular: ones on the diagonal, zeros above it.
All inputs are finite; a program needn't handle non-finite values.
Results may differ from a plain program's by a relative error of at most 0.00015.
Values sent between devices are 32-bit elements; how exact they have to be, the bound alone decides.
A program may use at most 192 MiB of HBM per device.

v0:
```python
import jax
import jax.numpy as jnp
from jax import lax
from jax.sharding import PartitionSpec as P

CAP = 2
precise = lax.Precision.HIGHEST


def broadcast(block, axis, holder):
    block = jnp.where(lax.axis_index(axis) == holder, block, jnp.zeros_like(block))
    return lax.psum(block, axis)


def pair_scale(scaled, pair_bits, diag_part, off_part):
    coupled = pair_bits.astype(jnp.float32) * off_part
    zero_col = jnp.zeros_like(scaled[:, :1])
    shifted_next = jnp.concatenate([scaled[:, 1:], zero_col], axis=1)
    shifted_prev = jnp.concatenate([zero_col, scaled[:, :-1]], axis=1)
    coupled_prev = jnp.concatenate([jnp.zeros_like(coupled[:1]), coupled[:-1]])
    return scaled * diag_part + shifted_next * coupled + shifted_prev * coupled_prev


def select_columns(matrix, wanted, anchor):
    block_width = matrix.shape[1]
    relative = wanted - anchor
    inside = (relative >= 0) & (relative < block_width)
    clipped = jnp.clip(relative, 0, block_width - 1)
    return jnp.where(inside[None, :], jnp.take(matrix, clipped, axis=1), 0.0)


def select_rows(matrix, wanted, anchor):
    block_height = matrix.shape[0]
    relative = wanted - anchor
    inside = (relative >= 0) & (relative < block_height)
    clipped = jnp.clip(relative, 0, block_height - 1)
    return jnp.where(inside[:, None], jnp.take(matrix, clipped, axis=0), 0.0)


def body(front, delayed, dest, pivots, pair_flags, linv, dinv_diag, dinv_off):
    col_count = lax.axis_size("col")
    rows_blk, cols_blk = front.shape
    row_start = lax.axis_index("row") * rows_blk
    col_start = lax.axis_index("col") * cols_blk
    panel_count = linv.shape[0]
    panel_width = linv.shape[1]
    slot_total = pivots.shape[0]
    slot_ids = jnp.arange(slot_total, dtype=jnp.int32)
    owner_ids = jnp.arange(col_count, dtype=jnp.int32)
    slot_hit = dest[:, None] == slot_ids[None, :]
    targets = jnp.sum(jnp.where(slot_hit, pivots[None, :], 0), axis=1)
    owners = targets // cols_blk
    within = targets - owners * cols_blk
    owner_hit = (owners[:, None] == owner_ids[None, :]).astype(jnp.int32)
    earlier = jnp.cumsum(owner_hit, axis=0) - owner_hit
    rank_in = jnp.sum(earlier * owner_hit, axis=1)
    slot_pos = jnp.arange(CAP, dtype=jnp.int32)
    placed = (owner_hit[:, :, None] > 0) & (rank_in[:, None, None] == slot_pos[None, None, :])
    send_vals = jnp.einsum("kos,kr->osr", placed.astype(jnp.float32), delayed, precision=precise)
    send_cols = jnp.sum(jnp.where(placed, within[:, None, None] + 1, 0), axis=0) - 1
    recv_vals, recv_cols = (
        lax.all_to_all(send_vals, "col", split_axis=0, concat_axis=0, tiled=True),
        lax.all_to_all(send_cols, "col", split_axis=0, concat_axis=0, tiled=True),
    )
    flat_vals = recv_vals.reshape(-1, rows_blk)
    flat_cols = recv_cols.reshape(-1)
    col_ids = jnp.arange(cols_blk, dtype=jnp.int32)
    col_hit = (flat_cols[:, None] == col_ids[None, :]).astype(jnp.float32)
    current = front + lax.dot_general(
        flat_vals, col_hit, (((0,), (0,)), ((), ())), precision=precise
    )
    factors = []
    piv_owner = pivots // cols_blk
    piv_hit = (piv_owner[:, None] == owner_ids[None, :]).astype(jnp.int32)
    piv_rank = jnp.sum((jnp.cumsum(piv_hit, axis=0) - piv_hit) * piv_hit, axis=1)
    per_owner = slot_total // col_count
    owned_here = piv_owner == lax.axis_index("col")
    rank_ids = jnp.arange(per_owner, dtype=jnp.int32)
    own_slots = jnp.sum(
        jnp.where(
            owned_here[None, :] & (piv_rank[None, :] == rank_ids[:, None]), slot_ids[None, :], 0
        ),
        axis=1,
    )
    compact = select_columns(current, pivots[own_slots], col_start)
    gathered = lax.all_gather(compact, "col", axis=1, tiled=True)
    every_panel = jnp.take(gathered, piv_owner * per_owner + piv_rank, axis=1)
    previous = []
    for panel_index in range(panel_count):
        offset = panel_index * panel_width
        panel_cols = every_panel[:, offset : offset + panel_width]
        for cols_before, rows_before in previous:
            panel_cols = panel_cols - lax.dot_general(
                cols_before,
                rows_before[offset : offset + panel_width],
                (((1,), (1,)), ((), ())),
                precision=precise,
            )
        finish_offset = panel_index * panel_width
        finish_scaled = jnp.dot(panel_cols, jnp.transpose(linv[panel_index]), precision=precise)
        finish_columns = pair_scale(
            finish_scaled,
            pair_flags[finish_offset : finish_offset + panel_width],
            dinv_diag[finish_offset : finish_offset + panel_width],
            dinv_off[finish_offset : finish_offset + panel_width],
        )
        root_row = col_start // rows_blk
        slice_start = jnp.clip(col_start - row_start, 0, rows_blk - cols_blk)
        root_piece = lax.dynamic_slice_in_dim(finish_scaled, slice_start, cols_blk, 0)
        col_scaled = broadcast(root_piece, "row", root_row)
        current = current - lax.dot_general(
            finish_columns, col_scaled, (((1,), (1,)), ((), ())), precision=precise
        )
        factors.append(finish_columns)
        if panel_index + 1 < panel_count:
            pivot_part = select_rows(finish_scaled, pivots, row_start)
            pivot_rows = lax.psum(pivot_part, "row")
            previous.append((finish_columns, pivot_rows))
    row_ids = row_start + jnp.arange(rows_blk, dtype=jnp.int32)
    row_in = jnp.any(row_ids[:, None] == pivots[None, :], axis=1)
    col_in = jnp.any((col_start + col_ids)[:, None] == pivots[None, :], axis=1)
    trailing = jnp.where(row_in[:, None] | col_in[None, :], 0.0, current)
    factor = jnp.concatenate(factors, axis=1)
    return (trailing, factor)


def solution(mesh):
    return jax.shard_map(
        body,
        mesh=mesh,
        in_specs=(P("row", "col"), P("col", "row"), P("col"), P(), P(), P(), P(), P()),
        out_specs=(P("row", "col"), P("row", None)),
        check_vma=False,
    )
```

profile of v0, /device:TPU:0, one launch (start us, length us, event | category | flops | bytes accessed | tf_op | source)
XLA Modules:
  0.0 721.7 jit_solution(9475887452106300543)
XLA Ops:
  9.2 7.3 %all-to-all-start.1 = ((s32[8,1,2]{2,1,0:T(1,128)}), s32[8,1,2]{2,1,0:T(1,128)S(1)}, u32[]{:S(2)}, u32[]{:S(2)}) async-start(s32[8,1,2]{2,1,0:T(1,128)} %copy.32), calls=%async_computation.1 | async-start | bytes 8192 | tf_op jit(solution)/shard_map/all_to_all | solution.py:63
  36.8 18.0 %convolution_add_fusion = f32[3072,1536]{1,0:T(8,128)} fusion(f32[3072,1536]{1,0:T(8,128)} %param.10, f32[16,3072]{1,0:T(8,128)S(1)} %reshape.189, s32[16]{0:T(128)S(1)} %eq.152), kind=kOutput, calls=%fused_computation.7 | convolution fusion | flops 910712832 | bytes 37945408 | tf_op jit(solution)/shard_map/dot_general | solution.py:69
  54.8 18.7 %copy.33 = f32[3072,1536]{0,1:T(8,128)} copy(f32[3072,1536]{1,0:T(8,128)} %convolution_add_fusion) | data formatting | bytes 37748736 | tf_op jit(solution)/shard_map/add | solution.py:69
  73.4 8.2 %gather_fusion.1 = f32[128,3072]{1,0:T(8,128)S(1)} fusion(f32[3072,1536]{0,1:T(8,128)} %copy.33, s32[1024]{0:T(1024)S(1)} %pad_clamp_fusion), kind=kCustom, calls=%fused_computation.4 | custom fusion | bytes 3146240 | tf_op jit(solution)/shard_map/jit(_take)/gather | solution.py:29
  84.1 173.5 %all-gather.2.cloned.1.call-done = f32[3072,1024]{0,1:T(8,128)} async-done(((f32[3072,128]{0,1:T(8,128)}), f32[3072,1024]{0,1:T(8,128)}) %all-gather.2.cloned.1.call-update) | async-done | bytes 12582928 | tf_op jit(solution)/shard_map/all_gather | solution.py:86
  257.6 16.5 %gather_fusion.2 = f32[1024,3072]{1,0:T(8,128)} fusion(f32[3072,1024]{0,1:T(8,128)} %all-gather.2.cloned.1.call-done, s32[1024]{0:T(1024)S(1)} %broadcast_clamp_fusion), kind=kCustom, calls=%fused_computation.5 | custom fusion | bytes 25169920 | tf_op jit(solution)/shard_map/jit(_take)/gather | solution.py:87
  274.1 12.6 %copy.34 = f32[1024,3072]{0,1:T(8,128)} copy(f32[1024,3072]{1,0:T(8,128)} %gather_fusion.2) | data formatting | bytes 25165824 | tf_op jit(solution)/shard_map/jit(_take)/gather | solution.py:87
  286.7 12.4 %select_bitcast_fusion = f32[3072,1024]{1,0:T(8,128)} fusion(f32[1024,3072]{0,1:T(8,128)} %copy.34, pred[1024]{0:T(1024)(128)(4,1)S(1)} %compare_and_fusion.2), kind=kLoop, calls=%fused_computation.9 | loop fusion | flops 3145728 | bytes 25166848 | tf_op jit(solution)/shard_map/jit(_take)/select_n | solution.py:87
  324.0 27.4 %all-reduce.14.cloned.1.call-done = f32[1024,256]{1,0:T(8,128)} async-done(((f32[1024,256]{1,0:T(8,128)}), f32[1024,256]{1,0:T(8,128)}) %all-reduce.14.cloned.1.call-update) | async-done | bytes 1048592 | tf_op jit(solution)/shard_map/psum | solution.py:117
  351.4 7.3 %convolution_subtract_fusion.5 = f32[3072,256]{1,0:T(8,128)S(1)} fusion(f32[3072,256]{0,1:T(8,128)S(1)} %multiply_add_fusion.3, f32[3072,1024]{1,0:T(8,128)} %select_bitcast_fusion, f32[1024,256]{1,0:T(8,128)} %all-reduce.14.cloned.1.call-done), kind=kOutput, calls=%fused_computation.17 | convolution fusion | flops 2416705536 | bytes 9699328 | tf_op jit(solution)/shard_map/dot_general | solution.py:93
  387.6 8.0 %convolution_subtract_fusion.4 = f32[3072,256]{1,0:T(8,128)} fusion(f32[3072,256]{0,1:T(8,128)S(1)} %multiply_add_fusion.3, f32[3072,1024]{1,0:T(8,128)} %select_bitcast_fusion, f32[1024,256]{1,0:T(8,128)S(1)} %copy-done.19), kind=kOutput, calls=%fused_computation.16 | convolution fusion | flops 2416705536 | bytes 9699328 | tf_op jit(solution)/shard_map/dot_general | solution.py:93
  397.3 8.3 %convolution_subtract_fusion.2 = f32[3072,256]{1,0:T(8,128)} fusion(f32[3072,256]{0,1:T(8,128)S(1)} %multiply_add_fusion.3, f32[3072,1024]{1,0:T(8,128)} %select_bitcast_fusion, f32[1024,256]{1,0:T(8,128)S(1)} %copy-done.19), kind=kOutput, calls=%fused_computation.14 | convolution fusion | flops 2416705536 | bytes 9699328 | tf_op jit(solution)/shard_map/dot_general | solution.py:93
  405.5 11.8 %all-reduce.16.cloned.1.call-done = f32[1024,256]{1,0:T(8,128)} async-done(((f32[1024,256]{1,0:T(8,128)}), f32[1024,256]{1,0:T(8,128)}) %all-reduce.16.cloned.1.call-update) | async-done | bytes 1048592 | tf_op jit(solution)/shard_map/psum | solution.py:117
  417.3 8.3 %convolution_subtract_fusion.3 = f32[3072,256]{1,0:T(8,128)S(1)} fusion(f32[3072,256]{1,0:T(8,128)} %convolution_subtract_fusion.4, f32[3072,256]{0,1:T(8,128)} %multiply_add_fusion.2, f32[1024,256]{1,0:T(8,128)} %all-reduce.16.cloned.1.call-done), kind=kOutput, calls=%fused_computation.15 | convolution fusion | flops 2416705536 | bytes 9699328 | tf_op jit(solution)/shard_map/dot_general | solution.py:93
  447.7 7.0 multiply_add_fusion.1
  457.2 8.1 %convolution_subtract_fusion.1 = f32[3072,256]{1,0:T(8,128)} fusion(f32[3072,256]{1,0:T(8,128)S(1)} %copy-done.16, f32[3072,256]{0,1:T(8,128)S(1)} %copy-done.8, f32[1024,256]{1,0:T(8,128)} %all-reduce.16.cloned.1.call-done), kind=kOutput, calls=%fused_computation.13 | convolution fusion | flops 2416705536 | bytes 9699328 | tf_op jit(solution)/shard_map/dot_general | solution.py:93
  465.3 19.0 %all-reduce.18.cloned.1.call-done = f32[1024,256]{1,0:T(8,128)} async-done(((f32[1024,256]{1,0:T(8,128)}), f32[1024,256]{1,0:T(8,128)}) %all-reduce.18.cloned.1.call-update) | async-done | bytes 1048592 | tf_op jit(solution)/shard_map/psum | solution.py:117
  484.4 8.3 %convolution_subtract_fusion = f32[3072,256]{1,0:T(8,128)S(1)} fusion(f32[3072,256]{1,0:T(8,128)} %convolution_subtract_fusion.1, f32[3072,256]{0,1:T(8,128)} %multiply_add_fusion.1, f32[1024,256]{1,0:T(8,128)} %all-reduce.18.cloned.1.call-done), kind=kOutput, calls=%fused_computation.12 | convolution fusion | flops 2416705536 | bytes 9699328 | tf_op jit(solution)/shard_map/dot_general | solution.py:93
  517.4 12.6 %copy.38 = f32[3072,1024]{1,0:T(8,128)} copy(f32[3072,1024]{0,1:T(8,128)} %pad_maximum_fusion) | data formatting | bytes 25165824
  530.0 90.6 %all-reduce.20.cloned.1.call-done = (f32[1536,256]{0,1:T(8,128)}, f32[1536,256]{0,1:T(8,128)}, f32[1536,256]{0,1:T(8,128)}, f32[1536,256]{0,1:T(8,128)}) async-done(((f32[1536,256]{0,1:T(8,128)}, f32[1536,256]{0,1:T(8,128)}, f32[1536,256]{0,1:T(8,128)}, f32[1536,256]{0,1:T(8,128)}), (f32[1536,256]{0,1:T(8,128)}, f32[1536,256]{0,1:T(8,128)}, f32[1536,256]{0,1:T(8,128)}, ...) | async-done | bytes 6291472 | tf_op jit(solution)/shard_map/psum | solution.py:12
  620.6 19.9 %fusion.44 = f32[3072,1536]{1,0:T(8,128)} fusion(f32[3072,256]{0,1:T(8,128)} %multiply_add_fusion.1, f32[1536,256]{0,1:T(8,128)} %get-tuple-element.11), kind=kOutput, calls=%fused_computation.119 | convolution fusion | flops 14495514624 | bytes 23592960 | tf_op jit(solution)/shard_map/dot_general | solution.py:111
  640.5 18.5 %fusion.43 = f32[3072,1536]{1,0:T(8,128)} fusion(f32[3072,256]{0,1:T(8,128)S(1)} %copy-done.10, f32[1536,256]{0,1:T(8,128)S(1)} %copy-done.18), kind=kOutput, calls=%fused_computation.118 | convolution fusion | flops 14495514624 | bytes 23592960 | tf_op jit(solution)/shard_map/dot_general | solution.py:111
  659.0 17.9 %fusion.42 = f32[3072,1536]{1,0:T(8,128)} fusion(f32[3072,256]{0,1:T(8,128)S(1)} %multiply_add_fusion.3, f32[1536,256]{0,1:T(8,128)S(1)} %copy-done.17), kind=kOutput, calls=%fused_computation.117 | convolution fusion | flops 14495514624 | bytes 23592960 | tf_op jit(solution)/shard_map/dot_general | solution.py:111
  676.9 38.1 %subtract_select_fusion = f32[3072,1536]{1,0:T(8,128)} fusion(f32[3072,1536]{1,0:T(8,128)} %fusion.44, f32[3072,1536]{1,0:T(8,128)} %fusion.43, f32[3072,1536]{1,0:T(8,128)} %convolution_add_fusion, f32[3072,1536]{1,0:T(8,128)} %fusion.42, f32[3072,256]{0,1:T(8,128)} %copy-done.15, f32[1536,256]{0,1:T(8,128)} %get-tuple-element.14, ...), kind=kOutput, calls=%fused_computation.6 | convolution fusion | flops 14523826176 | bytes 99095040 | tf_op jit(solution)/shard_map/dot_general | solution.py:111
  (126 shorter events, 129.0 us)
Async XLA Ops:
  7.2 9.3 %copy-start = (f32[8,3072]{1,0:T(8,128)S(1)}, f32[8,3072]{1,0:T(8,128)}, u32[]{:S(2)}) copy-start(f32[8,3072]{1,0:T(8,128)} %param.11) | copy-start | bytes 294916
  9.2 13.7 %all-to-all-start.1 = ((s32[8,1,2]{2,1,0:T(1,128)}), s32[8,1,2]{2,1,0:T(1,128)S(1)}, u32[]{:S(2)}, u32[]{:S(2)}) async-start(s32[8,1,2]{2,1,0:T(1,128)} %copy.32), calls=%async_computation.1 | async-start | bytes 8192 | tf_op jit(solution)/shard_map/all_to_all | solution.py:63
  22.9 13.8 %all-to-all-start = ((f32[8,2,3072]{2,1,0:T(2,128)}), f32[8,2,3072]{2,1,0:T(2,128)S(1)}, u32[]{:S(2)}, u32[]{:S(2)}) async-start(f32[8,2,3072]{2,1,0:T(2,128)} %copy.31), calls=%async_computation | async-start | bytes 393216 | tf_op jit(solution)/shard_map/all_to_all | solution.py:62
  28.9 228.7 %all-gather.2.cloned.1.call-start = ((), (), s32[]{:S(2)}) async-start(), calls=%async_computation.2 | async-start | bytes 14155776 | tf_op jit(solution)/shard_map/all_gather | solution.py:86
  81.7 2.3 copy-start.11
  81.7 2.3 copy-start.22
  83.2 268.2 %all-reduce.14.cloned.1.call-start = ((), (), s32[]{:S(2)}) async-start(), calls=%async_computation.3 | async-start | bytes 2097152 | tf_op jit(solution)/shard_map/psum | solution.py:117
  304.0 3.7 copy-start.6
  316.7 100.6 %all-reduce.16.cloned.1.call-start = ((), (), s32[]{:S(2)}) async-start(), calls=%async_computation.4 | async-start | bytes 2097152 | tf_op jit(solution)/shard_map/psum | solution.py:117
  316.9 5.4 copy-start.7
  380.4 103.9 %all-reduce.18.cloned.1.call-start = ((), (), s32[]{:S(2)}) async-start(), calls=%async_computation.5 | async-start | bytes 2097152 | tf_op jit(solution)/shard_map/psum | solution.py:117
  380.7 7.0 copy-start.19
  387.6 8.0 %copy-start.5 = (f32[3072,256]{0,1:T(8,128)S(1)}, f32[3072,256]{0,1:T(8,128)}, u32[]{:S(2)}) copy-start(f32[3072,256]{0,1:T(8,128)} %copy-done.4) | copy-start | bytes 9437188
  447.5 173.2 %all-reduce.20.cloned.1.call-start = ((), (), s32[]{:S(2)}) async-start(), calls=%async_computation.6 | async-start | bytes 12582912 | tf_op jit(solution)/shard_map/psum | solution.py:12
  447.7 7.1 copy-start.3
  447.7 8.7 %copy-start.16 = (f32[3072,256]{1,0:T(8,128)S(1)}, f32[3072,256]{1,0:T(8,128)}, u32[]{:S(2)}) copy-start(f32[3072,256]{1,0:T(8,128)} %convolution_subtract_fusion.2) | copy-start | bytes 9437188
  454.7 2.5 copy-start.8
  503.4 4.6 copy-start.13
  508.0 3.0 copy-start.9
  508.0 4.0 copy-start.14
  620.6 19.9 %copy-start.10 = (f32[3072,256]{0,1:T(8,128)S(1)}, f32[3072,256]{0,1:T(8,128)}, u32[]{:S(2)}) copy-start(f32[3072,256]{0,1:T(8,128)} %multiply_add_fusion.2) | copy-start | bytes 9437188
  620.6 19.9 %copy-start.18 = (f32[1536,256]{0,1:T(8,128)S(1)}, f32[1536,256]{0,1:T(8,128)}, u32[]{:S(2)}) copy-start(f32[1536,256]{0,1:T(8,128)} %get-tuple-element.12) | copy-start | bytes 4718596
  640.5 18.5 %copy-start.17 = (f32[1536,256]{0,1:T(8,128)S(1)}, f32[1536,256]{0,1:T(8,128)}, u32[]{:S(2)}) copy-start(f32[1536,256]{0,1:T(8,128)} %get-tuple-element.13) | copy-start | bytes 4718596
  676.9 38.1 %copy-start.1 = (f32[8,3072]{1,0:T(8,128)S(1)}, f32[8,3072]{1,0:T(8,128)}, u32[]{:S(2)}) copy-start(f32[8,3072]{1,0:T(8,128)} %param.11) | copy-start | bytes 294916
  (6 other events, 10.8 us)
Sparse Core Ops, SparseCore 0:
  83.3 174.2 all-gather.1
  316.8 34.4 all-reduce.13
  380.5 36.7 all-reduce.15
  447.6 36.7 all-reduce.17
  500.5 120.0 all-reduce.19
where the time goes:
time: 728 us; the launch traced here: 722 us
  waiting for transfers between devices  329 us (45%)
  matrix products  178 us (24%)
  local copies, waits for them, and re-layouts  124 us (17%)
  other arithmetic  61.7 us (8%)
  starting transfers between devices  14.6 us (2%)
  between operations  14.4 us (2%)
    all_gather x1, waiting for transfers between devices, body(): gathered = lax.all_gather(compact, 'col', axis=1, tiled=True)  174 us
    dot_general x4, matrix products, body(): lax.dot_general(finish_columns, col_scaled, (((1,), (1,)), ((), ())), pre...  94.3 us
    psum x1, waiting for transfers between devices, broadcast(): return lax.psum(block, axis)  90.6 us
    psum x3, waiting for transfers between devices, body(): pivot_rows = lax.psum(pivot_part, 'row')  58.2 us
    dot_general x6, matrix products, body(): lax.dot_general(cols_before, rows_before[offset:offset + panel_width], ((...  48.4 us
    gather x2, local copies, waits for them, and re-layouts, body(): every_panel = jnp.take(gathered, piv_owner * per_owner + piv_rank, axis=1)  29.1 us
    unnamed x47, local copies, waits for them, and re-layouts  21.9 us
    add x4, other arithmetic, pair_scale(): scaled * diag_part + shifted_next * coupled + shifted_prev * coupled_prev  20.7 us
  transfers between devices with their start and end apart: 7, of which 6 were waited for; matrix products, arithmetic and copies ran while one was open for 11% of the time, Pallas kernels for 0%

commit v1 on v0

--- a/solution.py
+++ b/solution.py
@@ -83,7 +83,12 @@
         axis=1,
     )
     compact = select_columns(current, pivots[own_slots], col_start)
-    gathered = lax.all_gather(compact, "col", axis=1, tiled=True)
+    ring = [compact]
+    for hop in range(7):
+        ring.append(lax.ppermute(ring[-1], "col", [(dev, (dev + 1) % 8) for dev in range(8)]))
+    gathered = jnp.roll(
+        jnp.concatenate(ring[::-1], axis=1), (lax.axis_index("col") + 1) * ring[0].shape[1], axis=1
+    )
     every_panel = jnp.take(gathered, piv_owner * per_owner + piv_rank, axis=1)
     previous = []
     for panel_index in range(panel_count):

time: 728 us -> 837 us (1.15)
  waiting for transfers between devices: 329 us -> 393 us
  local copies, waits for them, and re-layouts: 124 us -> 165 us
    ppermute x0 -> x7, waiting for transfers between devices: none -> 241 us  [body(): lax.ppermute(ring[-1], 'col', [(dev, (dev + 1) % 8) for dev in range(8)])]
    all_gather x1 -> x0, waiting for transfers between devices: 174 us -> none  [body(): gathered = lax.all_gather(compact, 'col', axis=1, tiled=True)]
    unnamed x47 -> x77, local copies, waits for them, and re-layouts: 21.9 us -> 50.9 us
    dynamic_slice x0 -> x1, local copies, waits for them, and re-layouts: none -> 11 us  [body(): jnp.roll(jnp.concatenate(ring[::-1], axis=1), (lax.axis_index('col') + 1)...]
  transfers between devices with their start and end apart: 7 -> 13, of which waited for: 6 -> 12; matrix products, arithmetic and copies ran while one was open for 11% -> 10% of each run, Pallas kernels for 0% -> 0%
where the time goes in v1:
time: 837 us; the launch traced here: 830 us
  waiting for transfers between devices  393 us (47%)
  matrix products  178 us (21%)
  local copies, waits for them, and re-layouts  165 us (20%)
  other arithmetic  64 us (8%)
  starting transfers between devices  15.4 us (2%)
  between operations  14.4 us (2%)
    ppermute x7, waiting for transfers between devices, body(): lax.ppermute(ring[-1], 'col', [(dev, (dev + 1) % 8) for dev in range(8)])  241 us
    dot_general x4, matrix products, body(): lax.dot_general(finish_columns, col_scaled, (((1,), (1,)), ((), ())), pre...  94.2 us
    psum x1, waiting for transfers between devices, broadcast(): return lax.psum(block, axis)  89.8 us
    psum x3, waiting for transfers between devices, body(): pivot_rows = lax.psum(pivot_part, 'row')  57.2 us
    unnamed x77, local copies, waits for them, and re-layouts  50.9 us
    dot_general x6, matrix products, body(): lax.dot_general(cols_before, rows_before[offset:offset + panel_width], ((...  48.1 us
    gather x2, local copies, waits for them, and re-layouts, body(): every_panel = jnp.take(gathered, piv_owner * per_owner + piv_rank, axis=1)  29.2 us
    add x4, other arithmetic, pair_scale(): scaled * diag_part + shifted_next * coupled + shifted_prev * coupled_prev  20.7 us
  transfers between devices with their start and end apart: 13, of which 12 were waited for; matrix products, arithmetic and copies ran while one was open for 10% of the time, Pallas kernels for 0%

profile of v1, /device:TPU:0, one launch (start us, length us, event | category | flops | bytes accessed | tf_op | source)
XLA Modules:
  0.0 830.0 jit_solution(8060164370416268573)
XLA Ops:
  36.8 18.0 %convolution_add_fusion = f32[3072,1536]{1,0:T(8,128)} fusion(f32[3072,1536]{1,0:T(8,128)} %param.10, f32[16,3072]{1,0:T(8,128)S(1)} %reshape.189, s32[16]{0:T(128)S(1)} %eq.155), kind=kOutput, calls=%fused_computation.7 | convolution fusion | flops 910712832 | bytes 37945408 | tf_op jit(solution)/shard_map/dot_general | solution.py:69
  54.8 18.7 %copy.33 = f32[3072,1536]{0,1:T(8,128)} copy(f32[3072,1536]{1,0:T(8,128)} %convolution_add_fusion) | data formatting | bytes 37748736 | tf_op jit(solution)/shard_map/add | solution.py:69
  83.0 35.9 %collective-permute-done = f32[3072,128]{0,1:T(8,128)S(1)} collective-permute-done((f32[3072,128]{0,1:T(8,128)S(1)}, f32[3072,128]{0,1:T(8,128)S(1)}, u32[]{:S(2)}, u32[]{:S(2)}) %collective-permute-start) | collective-permute-done | bytes 1572896 | tf_op jit(solution)/shard_map/ppermute | solution.py:88
  118.9 36.0 %collective-permute-done.1 = f32[3072,128]{0,1:T(8,128)S(1)} collective-permute-done((f32[3072,128]{0,1:T(8,128)S(1)}, f32[3072,128]{0,1:T(8,128)S(1)}, u32[]{:S(2)}, u32[]{:S(2)}) %collective-permute-start.1) | collective-permute-done | bytes 1572896 | tf_op jit(solution)/shard_map/ppermute | solution.py:88
  156.1 35.1 %collective-permute-done.2 = f32[3072,128]{0,1:T(8,128)S(1)} collective-permute-done((f32[3072,128]{0,1:T(8,128)S(1)}, f32[3072,128]{0,1:T(8,128)S(1)}, u32[]{:S(2)}, u32[]{:S(2)}) %collective-permute-start.2) | collective-permute-done | bytes 1572896 | tf_op jit(solution)/shard_map/ppermute | solution.py:88
  192.4 34.3 %collective-permute-done.3 = f32[3072,128]{0,1:T(8,128)S(1)} collective-permute-done((f32[3072,128]{0,1:T(8,128)S(1)}, f32[3072,128]{0,1:T(8,128)S(1)}, u32[]{:S(2)}, u32[]{:S(2)}) %collective-permute-start.3) | collective-permute-done | bytes 1572896 | tf_op jit(solution)/shard_map/ppermute | solution.py:88
  227.8 33.4 %collective-permute-done.4 = f32[3072,128]{0,1:T(8,128)S(1)} collective-permute-done((f32[3072,128]{0,1:T(8,128)S(1)}, f32[3072,128]{0,1:T(8,128)S(1)}, u32[]{:S(2)}, u32[]{:S(2)}) %collective-permute-start.4) | collective-permute-done | bytes 1572896 | tf_op jit(solution)/shard_map/ppermute | solution.py:88
  262.3 34.2 %collective-permute-done.5 = f32[3072,128]{0,1:T(8,128)} collective-permute-done((f32[3072,128]{0,1:T(8,128)S(1)}, f32[3072,128]{0,1:T(8,128)}, u32[]{:S(2)}, u32[]{:S(2)}) %collective-permute-start.5) | collective-permute-done | bytes 1572896 | tf_op jit(solution)/shard_map/ppermute | solution.py:88
  297.0 31.7 %collective-permute-done.6 = f32[3072,128]{0,1:T(8,128)} collective-permute-done((f32[3072,128]{0,1:T(8,128)}, f32[3072,128]{0,1:T(8,128)}, u32[]{:S(2)}, u32[]{:S(2)}) %collective-permute-start.6) | collective-permute-done | bytes 1572896 | tf_op jit(solution)/shard_map/ppermute | solution.py:88
  355.6 11.0 %constant_dynamic-slice_fusion = f32[3072,1024]{0,1:T(8,128)} fusion(f32[3072,2048]{0,1:T(8,128)} %constant_dynamic-update-slice_fusion, s32[]{:T(128)S(6)} %select_n.148), kind=kLoop, calls=%fused_computation.118 | loop fusion | bytes 25165828 | tf_op jit(solution)/shard_map/jit(_roll_dynamic)/dynamic_slice | solution.py:89
  366.6 16.6 %gather_fusion.2 = f32[1024,3072]{1,0:T(8,128)} fusion(f32[3072,1024]{0,1:T(8,128)} %constant_dynamic-slice_fusion, s32[1024]{0:T(1024)S(1)} %broadcast_clamp_fusion), kind=kCustom, calls=%fused_computation.5 | custom fusion | bytes 25169920 | tf_op jit(solution)/shard_map/jit(_take)/gather | solution.py:92
  383.2 12.6 %copy.34 = f32[1024,3072]{0,1:T(8,128)} copy(f32[1024,3072]{1,0:T(8,128)} %gather_fusion.2) | data formatting | bytes 25165824 | tf_op jit(solution)/shard_map/jit(_take)/gather | solution.py:92
  395.8 12.4 %select_bitcast_fusion = f32[3072,1024]{1,0:T(8,128)} fusion(f32[1024,3072]{0,1:T(8,128)} %copy.34, pred[1024]{0:T(1024)(128)(4,1)S(1)} %compare_and_fusion.2), kind=kLoop, calls=%fused_computation.9 | loop fusion | flops 3145728 | bytes 25166848 | tf_op jit(solution)/shard_map/jit(_take)/select_n | solution.py:92
  433.2 26.4 %all-reduce.14.cloned.1.call-done = f32[1024,256]{1,0:T(8,128)} async-done(((f32[1024,256]{1,0:T(8,128)}), f32[1024,256]{1,0:T(8,128)}) %all-reduce.14.cloned.1.call-update) | async-done | bytes 1048592 | tf_op jit(solution)/shard_map/psum | solution.py:122
  513.8 11.8 %all-reduce.16.cloned.1.call-done = f32[1024,256]{1,0:T(8,128)} async-done(((f32[1024,256]{1,0:T(8,128)}), f32[1024,256]{1,0:T(8,128)}) %all-reduce.16.cloned.1.call-update) | async-done | bytes 1048592 | tf_op jit(solution)/shard_map/psum | solution.py:122
  525.6 8.3 %convolution_subtract_fusion.3 = f32[3072,256]{1,0:T(8,128)S(1)} fusion(f32[3072,256]{1,0:T(8,128)} %convolution_subtract_fusion.4, f32[3072,256]{0,1:T(8,128)} %multiply_add_fusion.2, f32[1024,256]{1,0:T(8,128)} %all-reduce.16.cloned.1.call-done), kind=kOutput, calls=%fused_computation.15 | convolution fusion | flops 2416705536 | bytes 9699328 | tf_op jit(solution)/shard_map/dot_general | solution.py:98
  573.6 19.0 %all-reduce.18.cloned.1.call-done = f32[1024,256]{1,0:T(8,128)} async-done(((f32[1024,256]{1,0:T(8,128)}), f32[1024,256]{1,0:T(8,128)}) %all-reduce.18.cloned.1.call-update) | async-done | bytes 1048592 | tf_op jit(solution)/shard_map/psum | solution.py:122
  592.6 8.3 %convolution_subtract_fusion = f32[3072,256]{1,0:T(8,128)S(1)} fusion(f32[3072,256]{1,0:T(8,128)} %convolution_subtract_fusion.1, f32[3072,256]{0,1:T(8,128)} %multiply_add_fusion.1, f32[1024,256]{1,0:T(8,128)} %all-reduce.18.cloned.1.call-done), kind=kOutput, calls=%fused_computation.12 | convolution fusion | flops 2416705536 | bytes 9699328 | tf_op jit(solution)/shard_map/dot_general | solution.py:98
  626.5 12.7 %copy.38 = f32[3072,1024]{1,0:T(8,128)} copy(f32[3072,1024]{0,1:T(8,128)} %pad_maximum_fusion) | data formatting | bytes 25165824
  639.2 89.8 %all-reduce.20.cloned.1.call-done = (f32[1536,256]{0,1:T(8,128)}, f32[1536,256]{0,1:T(8,128)}, f32[1536,256]{0,1:T(8,128)}, f32[1536,256]{0,1:T(8,128)}) async-done(((f32[1536,256]{0,1:T(8,128)}, f32[1536,256]{0,1:T(8,128)}, f32[1536,256]{0,1:T(8,128)}, f32[1536,256]{0,1:T(8,128)}), (f32[1536,256]{0,1:T(8,128)}, f32[1536,256]{0,1:T(8,128)}, f32[1536,256]{0,1:T(8,128)}, ...) | async-done | bytes 6291472 | tf_op jit(solution)/shard_map/psum | solution.py:12
  729.0 19.9 %fusion.44 = f32[3072,1536]{1,0:T(8,128)} fusion(f32[3072,256]{0,1:T(8,128)} %multiply_add_fusion.1, f32[1536,256]{0,1:T(8,128)} %get-tuple-element.11), kind=kOutput, calls=%fused_computation.136 | convolution fusion | flops 14495514624 | bytes 23592960 | tf_op jit(solution)/shard_map/dot_general | solution.py:116
  748.9 18.3 %fusion.43 = f32[3072,1536]{1,0:T(8,128)} fusion(f32[3072,256]{0,1:T(8,128)S(1)} %copy-done.10, f32[1536,256]{0,1:T(8,128)S(1)} %copy-done.26), kind=kOutput, calls=%fused_computation.135 | convolution fusion | flops 14495514624 | bytes 23592960 | tf_op jit(solution)/shard_map/dot_general | solution.py:116
  767.2 18.0 %fusion.42 = f32[3072,1536]{1,0:T(8,128)} fusion(f32[3072,256]{0,1:T(8,128)S(1)} %multiply_add_fusion.3, f32[1536,256]{0,1:T(8,128)S(1)} %copy-done.25), kind=kOutput, calls=%fused_computation.134 | convolution fusion | flops 14495514624 | bytes 23592960 | tf_op jit(solution)/shard_map/dot_general | solution.py:116
  785.1 38.2 %subtract_select_fusion = f32[3072,1536]{1,0:T(8,128)} fusion(f32[3072,1536]{1,0:T(8,128)} %fusion.44, f32[3072,1536]{1,0:T(8,128)} %fusion.43, f32[3072,1536]{1,0:T(8,128)} %convolution_add_fusion, f32[3072,1536]{1,0:T(8,128)} %fusion.42, f32[3072,256]{0,1:T(8,128)} %copy-done.15, f32[1536,256]{0,1:T(8,128)} %get-tuple-element.14, ...), kind=kOutput, calls=%fused_computation.6 | convolution fusion | flops 14523826176 | bytes 99095040 | tf_op jit(solution)/shard_map/dot_general | solution.py:116
  (169 shorter events, 215.3 us)
Async XLA Ops:
  7.2 9.3 %copy-start = (f32[8,3072]{1,0:T(8,128)S(1)}, f32[8,3072]{1,0:T(8,128)}, u32[]{:S(2)}) copy-start(f32[8,3072]{1,0:T(8,128)} %param.11) | copy-start | bytes 294916
  9.2 13.7 %all-to-all-start.1 = ((s32[8,1,2]{2,1,0:T(1,128)}), s32[8,1,2]{2,1,0:T(1,128)S(1)}, u32[]{:S(2)}, u32[]{:S(2)}) async-start(s32[8,1,2]{2,1,0:T(1,128)} %copy.32), calls=%async_computation.1 | async-start | bytes 8192 | tf_op jit(solution)/shard_map/all_to_all | solution.py:63
  22.9 13.8 %all-to-all-start = ((f32[8,2,3072]{2,1,0:T(2,128)}), f32[8,2,3072]{2,1,0:T(2,128)S(1)}, u32[]{:S(2)}, u32[]{:S(2)}) async-start(f32[8,2,3072]{2,1,0:T(2,128)} %copy.31), calls=%async_computation | async-start | bytes 393216 | tf_op jit(solution)/shard_map/all_to_all | solution.py:62
  28.9 430.7 %all-reduce.14.cloned.1.call-start = ((), (), s32[]{:S(2)}) async-start(), calls=%async_computation.2 | async-start | bytes 2097152 | tf_op jit(solution)/shard_map/psum | solution.py:122
  81.7 215.1 %copy-start.28 = (f32[1024]{0:T(1024)S(1)}, f32[1024]{0:T(1024)}, u32[]{:S(2)}) copy-start(f32[1024]{0:T(1024)} %param.17) | copy-start | bytes 12292
  81.7 215.1 %copy-start.29 = (s32[1024]{0:T(1024)S(1)}, s32[1024]{0:T(1024)}, u32[]{:S(2)}) copy-start(s32[1024]{0:T(1024)} %param.14) | copy-start | bytes 12292
  81.7 215.2 %copy-start.30 = (f32[1024]{0:T(1024)S(1)}, f32[1024]{0:T(1024)}, u32[]{:S(2)}) copy-start(f32[1024]{0:T(1024)} %param.16) | copy-start | bytes 12292
  82.0 36.9 %collective-permute-start = (f32[3072,128]{0,1:T(8,128)S(1)}, f32[3072,128]{0,1:T(8,128)S(1)}, u32[]{:S(2)}, u32[]{:S(2)}) collective-permute-start(f32[3072,128]{0,1:T(8,128)S(1)} %select_bitcast_fusion.1), channel_id=1, source_target_pairs={{0,1},{1,2},{2,3},{3,4},{4,5},{5,6},{6,7},{7,0},{8,9},{9,10},{10,1... | collective-permute-start | bytes 4718600 | tf_op jit(solution)/shard_map/ppermute | solution.py:88
  118.9 36.0 %collective-permute-start.1 = (f32[3072,128]{0,1:T(8,128)S(1)}, f32[3072,128]{0,1:T(8,128)S(1)}, u32[]{:S(2)}, u32[]{:S(2)}) collective-permute-start(f32[3072,128]{0,1:T(8,128)S(1)} %collective-permute-done), channel_id=1, source_target_pairs={{0,1},{1,2},{2,3},{3,4},{4,5},{5,6},{6,7},{7,0},{8,9},{9,10},{10,1... | collective-permute-start | bytes 4718600 | tf_op jit(solution)/shard_map/ppermute | solution.py:88
  156.1 35.1 %collective-permute-start.2 = (f32[3072,128]{0,1:T(8,128)S(1)}, f32[3072,128]{0,1:T(8,128)S(1)}, u32[]{:S(2)}, u32[]{:S(2)}) collective-permute-start(f32[3072,128]{0,1:T(8,128)S(1)} %collective-permute-done.1), channel_id=1, source_target_pairs={{0,1},{1,2},{2,3},{3,4},{4,5},{5,6},{6,7},{7,0},{8,9},{9,10},{10,1... | collective-permute-start | bytes 4718600 | tf_op jit(solution)/shard_map/ppermute | solution.py:88
  192.4 34.3 %collective-permute-start.3 = (f32[3072,128]{0,1:T(8,128)S(1)}, f32[3072,128]{0,1:T(8,128)S(1)}, u32[]{:S(2)}, u32[]{:S(2)}) collective-permute-start(f32[3072,128]{0,1:T(8,128)S(1)} %collective-permute-done.2), channel_id=1, source_target_pairs={{0,1},{1,2},{2,3},{3,4},{4,5},{5,6},{6,7},{7,0},{8,9},{9,10},{10,1... | collective-permute-start | bytes 4718600 | tf_op jit(solution)/shard_map/ppermute | solution.py:88
  227.8 33.4 %collective-permute-start.4 = (f32[3072,128]{0,1:T(8,128)S(1)}, f32[3072,128]{0,1:T(8,128)S(1)}, u32[]{:S(2)}, u32[]{:S(2)}) collective-permute-start(f32[3072,128]{0,1:T(8,128)S(1)} %collective-permute-done.3), channel_id=1, source_target_pairs={{0,1},{1,2},{2,3},{3,4},{4,5},{5,6},{6,7},{7,0},{8,9},{9,10},{10,1... | collective-permute-start | bytes 4718600 | tf_op jit(solution)/shard_map/ppermute | solution.py:88
  262.3 34.2 %collective-permute-start.5 = (f32[3072,128]{0,1:T(8,128)S(1)}, f32[3072,128]{0,1:T(8,128)}, u32[]{:S(2)}, u32[]{:S(2)}) collective-permute-start(f32[3072,128]{0,1:T(8,128)S(1)} %collective-permute-done.4), channel_id=1, source_target_pairs={{0,1},{1,2},{2,3},{3,4},{4,5},{5,6},{6,7},{7,0},{8,9},{9,10},{10,1... | collective-permute-start | bytes 4718600 | tf_op jit(solution)/shard_map/ppermute | solution.py:88
  296.5 32.2 %collective-permute-start.6 = (f32[3072,128]{0,1:T(8,128)}, f32[3072,128]{0,1:T(8,128)}, u32[]{:S(2)}, u32[]{:S(2)}) collective-permute-start(f32[3072,128]{0,1:T(8,128)} %collective-permute-done.5), channel_id=1, source_target_pairs={{0,1},{1,2},{2,3},{3,4},{4,5},{5,6},{6,7},{7,0},{8,9},{9,10},{10,1... | collective-permute-start | bytes 4718600 | tf_op jit(solution)/shard_map/ppermute | solution.py:88
  297.0 37.2 %copy-start.24 = (f32[3072,128]{0,1:T(8,128)S(1)}, f32[3072,128]{0,1:T(8,128)}, u32[]{:S(2)}) copy-start(f32[3072,128]{0,1:T(8,128)} %copy-done.23) | copy-start | bytes 4718596
  425.8 99.7 %all-reduce.16.cloned.1.call-start = ((), (), s32[]{:S(2)}) async-start(), calls=%async_computation.3 | async-start | bytes 2097152 | tf_op jit(solution)/shard_map/psum | solution.py:122
  488.7 103.9 %all-reduce.18.cloned.1.call-start = ((), (), s32[]{:S(2)}) async-start(), calls=%async_computation.4 | async-start | bytes 2097152 | tf_op jit(solution)/shard_map/psum | solution.py:122
  496.1 8.0 copy-start.7
  555.7 173.3 %all-reduce.20.cloned.1.call-start = ((), (), s32[]{:S(2)}) async-start(), calls=%async_computation.5 | async-start | bytes 12582912 | tf_op jit(solution)/shard_map/psum | solution.py:12
  556.0 8.7 %copy-start.16 = (f32[3072,256]{1,0:T(8,128)S(1)}, f32[3072,256]{1,0:T(8,128)}, u32[]{:S(2)}) copy-start(f32[3072,256]{1,0:T(8,128)} %convolution_subtract_fusion.2) | copy-start | bytes 9437188
  729.0 19.9 %copy-start.10 = (f32[3072,256]{0,1:T(8,128)S(1)}, f32[3072,256]{0,1:T(8,128)}, u32[]{:S(2)}) copy-start(f32[3072,256]{0,1:T(8,128)} %multiply_add_fusion.2) | copy-start | bytes 9437188
  729.0 19.9 %copy-start.26 = (f32[1536,256]{0,1:T(8,128)S(1)}, f32[1536,256]{0,1:T(8,128)}, u32[]{:S(2)}) copy-start(f32[1536,256]{0,1:T(8,128)} %get-tuple-element.12) | copy-start | bytes 4718596
  748.9 18.3 %copy-start.25 = (f32[1536,256]{0,1:T(8,128)S(1)}, f32[1536,256]{0,1:T(8,128)}, u32[]{:S(2)}) copy-start(f32[1536,256]{0,1:T(8,128)} %get-tuple-element.13) | copy-start | bytes 4718596
  785.1 38.2 %copy-start.1 = (f32[8,3072]{1,0:T(8,128)S(1)}, f32[8,3072]{1,0:T(8,128)}, u32[]{:S(2)}) copy-start(f32[8,3072]{1,0:T(8,128)} %param.11) | copy-start | bytes 294916
  (20 other events, 59.0 us)
Sparse Core Ops, SparseCore 0:
  426.0 33.5 all-reduce.13
  488.8 36.7 all-reduce.15
  555.8 36.7 all-reduce.17
  608.9 120.0 all-reduce.19
